TPU v7x, 32 devices: a whole 2x2x4 slice. The times are simulated.
32 devices in a mesh: real: 4 (over z), rows: 4 (over y, core), field: 2 (over x).
Axes of the slice: x: 2, y: 2, z: 4, core: 2. Of those that a mesh axis runs over, the one named last changes fastest.
Arguments:
- sims: bfloat16 [4, 2, 2048, 2048], P('real', 'field', 'rows'), may hold values from -6 to 6
- data: bfloat16 [2, 2048, 2048], P('field', 'rows'), may hold values from -6 to 6
- mask_flags: int32 [16, 16], P('rows'), may hold values 0 or 1
- bins: int32 [512, 512], P(None, 'rows'), may hold values from 0 to 63
- cl_signal: float32 [2, 64], P('field'), may hold values from 0.5 to 4
- cl_noise: float32 [2, 64], P('field'), may hold values from 0.1 to 2
- norm: float32 [64], replicated, may hold values from 0.5 to 2
- matching: int32 [4], replicated, may hold values from 0 to 3, each once
Outputs:
- estimates: float32 [4, 2, 2, 512, 512], P('real', None, None, None, 'rows')
Inputs may be any that keep to these rules, and one draw needn't show every extreme that they name: `matching`: each realization index appears exactly once.
All inputs are finite; a program needn't handle non-finite values. No bound on the sum of `mask_flags` on one device may be relied on, other than what follows from the above.
Results may differ from a plain program's by a relative error of at most 0.011.
Values may be sent and summed in bfloat16 or wider, within the bound.
A program may use at most 128 MiB of HBM per device.

v0:
```python
import math
import jax
import jax.numpy as jnp
from jax import lax
from jax.sharding import PartitionSpec as P

TILE = 128


def tables(npix, kf, scale):
    pixel = jnp.arange(npix, dtype=jnp.int32)
    freq = jnp.arange(kf, dtype=jnp.int32) - kf // 2
    phase = jnp.mod(pixel[:, None] * freq[None, :], npix)
    angle = phase.astype(jnp.float32) * (2.0 * math.pi / npix)
    return (
        (jnp.cos(angle) * scale).astype(jnp.bfloat16),
        (jnp.sin(angle) * scale).astype(jnp.bfloat16),
    )


def expand_mask(flags, tile):
    first, second = flags.shape
    full = jnp.broadcast_to(flags[:, None, :, None], (first, tile, second, tile))
    return full.reshape(first * tile, second * tile) > 0


def column_part(maps, cos_t, sin_t):
    count, height, width = maps.shape
    flat = maps.reshape(count * height, width)
    a_re = (
        jnp.dot(flat, cos_t, preferred_element_type=jnp.float32)
        .astype(jnp.bfloat16)
        .reshape(count, height, -1)
    )
    a_im = (
        (-jnp.dot(flat, sin_t, preferred_element_type=jnp.float32))
        .astype(jnp.bfloat16)
        .reshape(count, height, -1)
    )
    return (a_re, a_im)


def row_part(a_re, a_im, cos_t, sin_t):
    a_re, a_im = (
        lax.all_to_all(a_re, "rows", split_axis=2, concat_axis=1, tiled=True),
        lax.all_to_all(a_im, "rows", split_axis=2, concat_axis=1, tiled=True),
    )
    x_re = jnp.einsum("yk,myj->mkj", cos_t, a_re, preferred_element_type=jnp.float32) + jnp.einsum(
        "yk,myj->mkj", sin_t, a_im, preferred_element_type=jnp.float32
    )
    x_im = jnp.einsum("yk,myj->mkj", cos_t, a_im, preferred_element_type=jnp.float32) - jnp.einsum(
        "yk,myj->mkj", sin_t, a_re, preferred_element_type=jnp.float32
    )
    return (x_re, x_im)


def inverse(z_re, z_im, icos, isin):
    count = z_re.shape[0]
    y_re = (
        jnp.einsum("yk,mkj->myj", icos, z_re, preferred_element_type=jnp.float32)
        - jnp.einsum("yk,mkj->myj", isin, z_im, preferred_element_type=jnp.float32)
    ).astype(jnp.bfloat16)
    y_im = (
        jnp.einsum("yk,mkj->myj", icos, z_im, preferred_element_type=jnp.float32)
        + jnp.einsum("yk,mkj->myj", isin, z_re, preferred_element_type=jnp.float32)
    ).astype(jnp.bfloat16)
    y_re, y_im = (
        lax.all_to_all(y_re, "rows", split_axis=1, concat_axis=2, tiled=True),
        lax.all_to_all(y_im, "rows", split_axis=1, concat_axis=2, tiled=True),
    )
    height = y_re.shape[1]
    flat_re = y_re.reshape(count * height, -1)
    flat_im = y_im.reshape(count * height, -1)
    out = jnp.dot(flat_re, icos.T, preferred_element_type=jnp.float32) - jnp.dot(
        flat_im, isin.T, preferred_element_type=jnp.float32
    )
    return out.astype(jnp.bfloat16).reshape(count, height, -1)


def filter_legs(x_re, x_im, wcell, gcell, lx, ly):
    grad_x = lx * gcell
    grad_y = ly * gcell
    z_re = jnp.stack([wcell * x_re, -grad_x * x_im, -grad_y * x_im])
    z_im = jnp.stack([wcell * x_im, grad_x * x_re, grad_y * x_re])
    return (z_re.astype(jnp.bfloat16), z_im.astype(jnp.bfloat16))


def select_rows(piece, partner_id):
    count = piece.shape[0]
    hit = jnp.arange(count, dtype=jnp.int32) == partner_id
    hit = hit.reshape((count,) + (1,) * (piece.ndim - 1))
    return jnp.sum(jnp.where(hit, piece, jnp.zeros_like(piece)), axis=0).astype(piece.dtype)


def lookup_cells(bins, values):
    nbins = values.shape[0]
    match_bin = bins[:, :, None] == jnp.arange(nbins, dtype=jnp.int32)[None, None, :]
    return jnp.sum(jnp.where(match_bin, values[None, None, :], jnp.zeros((), jnp.float32)), axis=2)


def body(sims, data, mask_flags, bins, cl_signal, cl_noise, norm, matching):
    npix = sims.shape[3]
    kf = bins.shape[0]
    cols = bins.shape[1]
    mask = expand_mask(mask_flags, TILE)
    stacked = jnp.concatenate([sims[0], data], axis=0)
    masked = jnp.where(mask[None], stacked, jnp.zeros_like(stacked))
    cos_t, sin_t = tables(npix, kf, npix ** (-0.5))
    icos, isin = tables(npix, kf, kf ** (-0.5))
    step_size = 2.0 * math.pi / npix
    col_freq = (lax.axis_index("rows") * cols + jnp.arange(cols, dtype=jnp.int32) - kf // 2).astype(
        jnp.float32
    ) * step_size
    row_freq = (jnp.arange(kf, dtype=jnp.int32) - kf // 2).astype(jnp.float32) * step_size
    lx = jnp.broadcast_to(col_freq[None, :], (kf, cols))
    ly = jnp.broadcast_to(row_freq[:, None], (kf, cols))
    weight_vals = 1.0 / (cl_signal[0] + cl_noise[0])
    grad_vals = cl_signal[0] * weight_vals
    wcell = lookup_cells(bins, weight_vals)
    gcell = lookup_cells(bins, grad_vals)
    ncell = lookup_cells(bins, norm)
    first_re, first_im = column_part(masked, cos_t, sin_t)
    x_re, x_im = row_part(first_re, first_im, cos_t, sin_t)
    own_re, own_im = filter_legs(x_re[0], x_im[0], wcell, gcell, lx, ly)
    dat_re, dat_im = filter_legs(x_re[1], x_im[1], wcell, gcell, lx, ly)
    legs = inverse(
        jnp.concatenate([own_re, dat_re], axis=0),
        jnp.concatenate([own_im, dat_im], axis=0),
        icos,
        isin,
    )
    sim_legs = legs[0:3]
    data_legs = legs[3:6].astype(jnp.float32)
    real_index = lax.axis_index("real")
    partner_id = jnp.sum(
        jnp.where(jnp.arange(matching.shape[0], dtype=jnp.int32) == real_index, matching, 0)
    )
    empty = jnp.zeros_like(x_re[0])
    p_re = empty + select_rows(
        lax.all_gather(x_re[0:1].astype(jnp.bfloat16), "real", axis=0, tiled=True).astype(
            jnp.float32
        ),
        partner_id,
    )
    p_im = empty + select_rows(
        lax.all_gather(x_im[0:1].astype(jnp.bfloat16), "real", axis=0, tiled=True).astype(
            jnp.float32
        ),
        partner_id,
    )
    z_re, z_im = filter_legs(p_re, p_im, wcell, gcell, lx, ly)
    partner_legs = inverse(z_re, z_im, icos, isin)
    own = sim_legs.astype(jnp.float32)
    other = partner_legs.astype(jnp.float32)
    ds_x = data_legs[1] * own[0] + own[1] * data_legs[0]
    ss_x = own[1] * other[0] + other[1] * own[0]
    ds_y = data_legs[2] * own[0] + own[2] * data_legs[0]
    ss_y = own[2] * other[0] + other[2] * own[0]
    products = jnp.stack([ds_x, ss_x, ds_y, ss_y]).astype(jnp.bfloat16)
    height = products.shape[1]
    mine = lax.all_to_all(products[None], "field", split_axis=1, concat_axis=0, tiled=True)
    sources = mine.shape[0]
    part_re, part_im = column_part(mine.reshape(sources * 2, height, npix), cos_t, sin_t)
    sum_re = jnp.sum(part_re.astype(jnp.float32).reshape(sources, 2, height, -1), axis=0)
    sum_im = jnp.sum(part_im.astype(jnp.float32).reshape(sources, 2, height, -1), axis=0)
    s_re, s_im = row_part(sum_re.astype(jnp.bfloat16), sum_im.astype(jnp.bfloat16), cos_t, sin_t)
    direction = jnp.where(lax.axis_index("field") == 0, lx, ly)
    scale = ncell * direction
    terms = jnp.stack([-scale * s_im, scale * s_re], axis=1)
    total = lax.psum(terms.astype(jnp.bfloat16), "field").astype(jnp.float32)
    return total[None]


def solution(mesh):
    in_specs = (
        P("real", "field", "rows", None),
        P("field", "rows", None),
        P("rows", None),
        P(None, "rows"),
        P("field", None),
        P("field", None),
        P(),
        P(),
    )
    out_specs = P("real", None, None, None, "rows")
    return jax.shard_map(body, mesh=mesh, in_specs=in_specs, out_specs=out_specs, check_vma=False)
```

profile of v0, /device:TPU:0, one launch (start us, length us, event | category | flops | bytes accessed | tf_op | source)
XLA Modules:
  0.0 774.8 jit_solution(14107730076439929142)
XLA Ops:
  10.6 16.8 %negate_convert_fusion.1 = bf16[1024,512]{1,0:T(8,128)(2,1)S(1)} fusion(bf16[1024,2048]{1,0:T(8,128)(2,1)S(1)} %bitcast.283, s32[512]{0:T(512)S(1)} %iota_add_fusion), kind=kOutput, calls=%fused_computation.84 | convolution fusion | flops 2165309440 | bytes 5244928 | tf_op jit(solution)/shard_map/dot_general | solution.py:36
  34.0 18.9 %fusion.65 = bf16[1024,512]{1,0:T(8,128)(2,1)S(1)} fusion(bf16[1024,2048]{1,0:T(8,128)(2,1)} %bitcast.284, s32[512]{0:T(512)S(1)} %iota_add_fusion), kind=kOutput, calls=%fused_computation.94 | convolution fusion | flops 2164785152 | bytes 5244928 | tf_op jit(solution)/shard_map/dot_general | solution.py:31
  55.7 16.3 %select_reduce_fusion.2 = (f32[512,128]{1,0:T(8,128)}, f32[512,128]{1,0:T(8,128)S(1)}, f32[512,128]{1,0:T(8,128)S(1)}) fusion(f32[64]{0:T(128)S(1)} %copy-done.12, s32[512,128]{1,0:T(8,128)S(1)} %copy-done.7, f32[64]{0:T(128)S(1)} %get-tuple-element.12, f32[64]{0:T(128)S(1)} %get-tuple-element.13), kind=kLoop, calls=%fused_computation.3 | loop fusion | flops 29163520 | bytes 1049344 | tf_op jit(solution)/shard_map/reduce_sum | solution.py:98
  80.3 16.7 %fusion.46 = f32[2,128,512]{2,1,0:T(8,128)} fusion(bf16[2,2048,128]{1,2,0:T(8,128)(2,1)S(1)} %all_to_all.110, s32[512]{0:T(512)S(1)} %iota_add_fusion), kind=kOutput, calls=%fused_computation.74 | convolution fusion | flops 553648128 | bytes 1574912 | tf_op jit(solution)/shard_map/yk,myj->mkj/dot_general | solution.py:48
  99.6 16.5 %fusion.44 = f32[2,128,512]{2,1,0:T(8,128)S(1)} fusion(bf16[2,2048,128]{1,2,0:T(8,128)(2,1)S(1)} %all_to_all.106, s32[512]{0:T(512)S(1)} %iota_add_fusion), kind=kOutput, calls=%fused_computation.72 | convolution fusion | flops 553648128 | bytes 1574912 | tf_op jit(solution)/shard_map/yk,myj->mkj/dot_general | solution.py:51
  116.1 17.2 %fusion.69 = f32[2,512,128]{1,2,0:T(8,128)S(1)} fusion(f32[2,128,512]{2,1,0:T(8,128)S(1)} %copy-done.16, bf16[2,2048,128]{1,2,0:T(8,128)(2,1)} %copy-done.6, s32[512]{0:T(512)S(1)} %iota_add_fusion), kind=kOutput, calls=%fused_computation.96 | convolution fusion | flops 553779200 | bytes 2099200 | tf_op jit(solution)/shard_map/yk,myj->mkj/dot_general | solution.py:48
  151.5 17.2 %all_gather.6 = bf16[4,512,128]{2,1,0:T(8,128)(2,1)S(1)} all-gather(bf16[1,512,128]{2,1,0:T(8,128)(2,1)S(1)} %copy.78), channel_id=1, replica_groups=mesh['real'=4,'rows'=4,'field'=2] {'real'}, dimensions={0}, use_global_device_ids=true | all-gather | bytes 655360 | tf_op jit(solution)/shard_map/all_gather | solution.py:140
  201.2 17.3 %fusion.32 = f32[3,128,2048]{2,1,0:T(8,128)} fusion(s32[512]{0:T(512)S(1)} %iota_add_fusion, bf16[1,512,128]{1,2,0:T(8,128)(2,1)S(1)} %get-tuple-element.34, bf16[1,512,128]{1,2,0:T(8,128)(2,1)S(1)} %get-tuple-element.35, bf16[1,512,128]{1,2,0:T(8,128)(2,1)S(1)} %get-tuple-element.37), kind=kOutput, calls=%fused_computation.60 | convolution fusion | flops 822476800 | bytes 3540992 | tf_op jit(solution)/shard_map/yk,mkj->myj/dot_general | solution.py:64
  218.5 16.7 %fusion.22 = bf16[3,2048,128]{1,2,0:T(8,128)(2,1)S(1)} fusion(f32[3,128,2048]{2,1,0:T(8,128)S(1)} %fusion.34, s32[512]{0:T(512)S(1)} %iota_add_fusion, bf16[1,512,128]{1,2,0:T(8,128)(2,1)S(1)} %get-tuple-element.34, bf16[1,512,128]{1,2,0:T(8,128)(2,1)S(1)} %get-tuple-element.35, bf16[1,512,128]{1,2,0:T(8,128)(2,1)S(1)} %get-tuple-element.37), kind=kOutput, calls=%fused_computation.50 | convolution fusion | flops 824049664 | bytes 5113856 | tf_op jit(solution)/shard_map/yk,mkj->myj/dot_general | solution.py:61
  241.6 18.6 %fusion.23 = bf16[3,2048,128]{1,2,0:T(8,128)(2,1)} fusion(f32[3,128,2048]{2,1,0:T(8,128)} %fusion.32, s32[512]{0:T(512)S(1)} %iota_add_fusion, bf16[1,512,128]{1,2,0:T(8,128)(2,1)S(1)} %get-tuple-element.25, bf16[1,512,128]{1,2,0:T(8,128)(2,1)S(1)} %get-tuple-element.24, bf16[1,512,128]{1,2,0:T(8,128)(2,1)S(1)} %get-tuple-element.36), kind=kOutput, calls=%fused_computation.51 | convolution fusion | flops 824049664 | bytes 5113856 | tf_op jit(solution)/shard_map/yk,mkj->myj/dot_general | solution.py:65
  267.7 20.1 %fusion.38 = f32[6,128,2048]{2,1,0:T(8,128)} fusion(bf16[6,512,128]{1,2,0:T(8,128)(2,1)} %get-tuple-element.33, s32[512]{0:T(512)S(1)} %iota_add_fusion), kind=kOutput, calls=%fused_computation.66 | convolution fusion | flops 1627389952 | bytes 7079936 | tf_op jit(solution)/shard_map/yk,mkj->myj/dot_general | solution.py:60
  293.8 20.4 %fusion.20 = bf16[6,2048,128]{1,2,0:T(8,128)(2,1)} fusion(f32[6,128,2048]{2,1,0:T(8,128)} %fusion.38, bf16[6,512,128]{1,2,0:T(8,128)(2,1)} %fusion.125, s32[512]{0:T(512)S(1)} %iota_add_fusion), kind=kOutput, calls=%fused_computation.47 | convolution fusion | flops 1630535680 | bytes 10225664 | tf_op jit(solution)/shard_map/yk,mkj->myj/dot_general | solution.py:61
  325.8 16.4 %fusion.36 = f32[6,128,2048]{2,1,0:T(8,128)S(1)} fusion(bf16[6,512,128]{1,2,0:T(8,128)(2,1)S(1)} %copy-done.9, s32[512]{0:T(512)S(1)} %iota_add_fusion), kind=kOutput, calls=%fused_computation.64 | convolution fusion | flops 1627389952 | bytes 7079936 | tf_op jit(solution)/shard_map/yk,mkj->myj/dot_general | solution.py:64
  342.3 22.0 %fusion.21 = bf16[6,2048,128]{1,2,0:T(8,128)(2,1)} fusion(f32[6,128,2048]{2,1,0:T(8,128)S(1)} %fusion.36, bf16[6,512,128]{1,2,0:T(8,128)(2,1)S(1)} %copy-done.11, s32[512]{0:T(512)S(1)} %iota_add_fusion), kind=kOutput, calls=%fused_computation.48 | convolution fusion | flops 1630535680 | bytes 10225664 | tf_op jit(solution)/shard_map/yk,mkj->myj/dot_general | solution.py:65
  375.2 20.1 %fusion.60 = f32[1536,2048]{1,0:T(8,128)} fusion(s32[512]{0:T(512)S(1)} %iota_add_fusion, bf16[192,8,4,128]{3,2,1,0:T(4,128)(2,1)S(1)} %bitcast.298), kind=kOutput, calls=%fused_computation.89 | convolution fusion | flops 3238002688 | bytes 14157824 | tf_op jit(solution)/shard_map/dot_general | solution.py:74
  400.2 22.3 %fusion = f32[1536,2048]{1,0:T(8,128)} fusion(f32[1536,2048]{1,0:T(8,128)} %fusion.60, s32[512]{0:T(512)S(1)} %iota_add_fusion, bf16[192,8,4,128]{3,2,1,0:T(4,128)(2,1)S(1)} %bitcast.297), kind=kOutput, calls=%fused_computation.7 | convolution fusion | flops 3247439872 | bytes 26740736 | tf_op jit(solution)/shard_map/dot_general | solution.py:74
  427.0 23.9 %fusion.17 = f32[3072,2048]{1,0:T(8,128)} fusion(bf16[384,8,4,128]{3,2,1,0:T(4,128)(2,1)S(1)} %bitcast.293, s32[512]{0:T(512)S(1)} %iota_add_fusion), kind=kOutput, calls=%fused_computation.42 | convolution fusion | flops 6459228160 | bytes 28313600 | tf_op jit(solution)/shard_map/dot_general | solution.py:74
  455.5 24.4 %subtract_convert_fusion = bf16[3072,2048]{1,0:T(8,128)(2,1)S(1)} fusion(f32[3072,2048]{1,0:T(8,128)} %fusion.17, bf16[384,8,4,128]{3,2,1,0:T(4,128)(2,1)S(1)} %bitcast.292, s32[512]{0:T(512)S(1)} %iota_add_fusion), kind=kOutput, calls=%fused_computation | convolution fusion | flops 6471811072 | bytes 40896512 | tf_op jit(solution)/shard_map/dot_general | solution.py:74
  517.6 93.2 %all-to-all-done.6 = bf16[1,4,512,2048]{3,2,0,1:T(8,128)(2,1)} async-done(((bf16[1,4,512,2048]{3,2,0,1:T(8,128)(2,1)}), bf16[1,4,512,2048]{3,2,0,1:T(8,128)(2,1)}, u32[]{:S(2)}, u32[]{:S(2)}) %all-to-all-start.6) | async-done | bytes 8388640 | tf_op jit(solution)/shard_map/all_to_all | solution.py:161
  610.8 21.3 %negate_convert_fusion = bf16[2048,512]{1,0:T(8,128)(2,1)S(1)} fusion(bf16[2048,2048]{1,0:T(8,128)(2,1)} %bitcast.37, s32[512]{0:T(512)S(1)} %iota_add_fusion), kind=kOutput, calls=%fused_computation.31 | convolution fusion | flops 4313841664 | bytes 10487808 | tf_op jit(solution)/shard_map/dot_general | solution.py:36
  639.1 22.1 %convolution_convert_fusion = bf16[2048,512]{1,0:T(8,128)(2,1)} fusion(bf16[2048,2048]{1,0:T(8,128)(2,1)} %bitcast.37, s32[512]{0:T(512)S(1)} %iota_add_fusion), kind=kOutput, calls=%fused_computation.49 | convolution fusion | flops 4312793088 | bytes 10487808 | tf_op jit(solution)/shard_map/dot_general | solution.py:31
  670.0 16.3 %fusion.40 = f32[2,128,512]{2,1,0:T(8,128)S(1)} fusion(bf16[2,2048,128]{1,2,0:T(8,128)(2,1)S(1)} %bitcast.299, s32[512]{0:T(512)S(1)} %iota_add_fusion), kind=kOutput, calls=%fused_computation.68 | convolution fusion | flops 553648128 | bytes 1574912 | tf_op jit(solution)/shard_map/yk,myj->mkj/dot_general | solution.py:48
  686.6 16.1 %fusion.42 = f32[2,128,512]{2,1,0:T(8,128)S(1)} fusion(bf16[2,2048,128]{1,2,0:T(8,128)(2,1)S(1)} %bitcast.301, s32[512]{0:T(512)S(1)} %iota_add_fusion), kind=kOutput, calls=%fused_computation.70 | convolution fusion | flops 553648128 | bytes 1574912 | tf_op jit(solution)/shard_map/yk,myj->mkj/dot_general | solution.py:51
  735.8 29.7 %all-reduce.2.cloned.1.call-done = bf16[1,2,2,512,128]{3,4,1,2,0:T(8,128)(2,1)} async-done(((bf16[1,2,2,512,128]{3,4,1,2,0:T(8,128)(2,1)}), bf16[1,2,2,512,128]{3,4,1,2,0:T(8,128)(2,1)}) %all-reduce.2.cloned.1.call-update) | async-done | bytes 524304 | tf_op jit(solution)/shard_map/psum | solution.py:170
  (114 shorter events, 220.0 us)
Async XLA Ops:
  6.5 1.8 copy-start.2
  10.6 16.8 %copy-start = (bf16[2,512,2048]{2,1,0:T(8,128)(2,1)}, bf16[2,512,2048]{2,1,0:T(8,128)(2,1)S(1)}, u32[]{:S(2)}) copy-start(bf16[2,512,2048]{2,1,0:T(8,128)(2,1)S(1)} %maximum_select_fusion) | copy-start | bytes 12582916
  29.5 42.5 %all-to-all-start.1 = ((bf16[2,512,512]{1,0,2:T(2,128)(2,1)}), bf16[2,512,512]{1,0,2:T(2,128)(2,1)S(1)}, u32[]{:S(2)}, u32[]{:S(2)}) async-start(bf16[2,512,512]{1,0,2:T(2,128)(2,1)} %copy.71), calls=%async_computation.1 | async-start | bytes 2097152 | tf_op jit(solution)/shard_map/all_to_all | solution.py:46
  33.9 21.0 %copy-start.13 = (f32[1,64]{1,0:T(1,128)S(1)}, f32[1,64]{1,0:T(1,128)}, u32[]{:S(2)}) copy-start(f32[1,64]{1,0:T(1,128)} %param.12) | copy-start | bytes 772
  33.9 21.0 %copy-start.14 = (f32[1,64]{1,0:T(1,128)S(1)}, f32[1,64]{1,0:T(1,128)}, u32[]{:S(2)}) copy-start(f32[1,64]{1,0:T(1,128)} %param.13) | copy-start | bytes 772
  34.0 21.0 %copy-start.15 = (s32[4]{0:T(128)S(1)}, s32[4]{0:T(128)}, u32[]{:S(2)}) copy-start(s32[4]{0:T(128)} %param.15) | copy-start | bytes 52
  34.0 21.7 %copy-start.7 = (s32[512,128]{1,0:T(8,128)S(1)}, s32[512,128]{1,0:T(8,128)}, u32[]{:S(2)}) copy-start(s32[512,128]{1,0:T(8,128)} %param.11) | copy-start | bytes 786436
  34.0 21.7 %copy-start.12 = (f32[64]{0:T(128)S(1)}, f32[64]{0:T(128)}, u32[]{:S(2)}) copy-start(f32[64]{0:T(128)} %param.14) | copy-start | bytes 772
  72.0 25.0 %all-to-all-start = ((bf16[2,512,512]{1,0,2:T(2,128)(2,1)}), bf16[2,512,512]{1,0,2:T(2,128)(2,1)S(1)}, u32[]{:S(2)}, u32[]{:S(2)}) async-start(bf16[2,512,512]{1,0,2:T(2,128)(2,1)} %copy.69), calls=%async_computation | async-start | bytes 2097152 | tf_op jit(solution)/shard_map/all_to_all | solution.py:45
  80.3 16.7 %copy-start.4 = (bf16[2,2048,128]{1,2,0:T(8,128)(2,1)}, bf16[2,2048,128]{1,2,0:T(8,128)(2,1)S(1)}, u32[]{:S(2)}) copy-start(bf16[2,2048,128]{1,2,0:T(8,128)(2,1)S(1)} %all_to_all.110) | copy-start | bytes 3145732
  99.6 16.5 %copy-start.16 = (f32[2,128,512]{2,1,0:T(8,128)S(1)}, f32[2,128,512]{2,1,0:T(8,128)}, u32[]{:S(2)}) copy-start(f32[2,128,512]{2,1,0:T(8,128)} %fusion.46) | copy-start | bytes 1572868
  116.1 17.3 %copy-start.5 = (bf16[2,2048,128]{1,2,0:T(8,128)(2,1)S(1)}, bf16[2,2048,128]{1,2,0:T(8,128)(2,1)}, u32[]{:S(2)}) copy-start(bf16[2,2048,128]{1,2,0:T(8,128)(2,1)} %copy-done.4) | copy-start | bytes 3145732
  149.2 35.8 %copy-start.1 = (f32[2,512,128]{1,2,0:T(8,128)}, f32[2,512,128]{1,2,0:T(8,128)S(1)}, u32[]{:S(2)}) copy-start(f32[2,512,128]{1,2,0:T(8,128)S(1)} %fusion.75) | copy-start | bytes 1572868
  237.8 50.1 %all-to-all-start.4 = ((bf16[3,2048,128]{2,0,1:T(4,128)(2,1)}), bf16[3,2048,128]{2,0,1:T(4,128)(2,1)S(1)}, u32[]{:S(2)}, u32[]{:S(2)}) async-start(bf16[3,2048,128]{2,0,1:T(4,128)(2,1)} %copy.82), calls=%async_computation.4 | async-start | bytes 4194304 | tf_op jit(solution)/shard_map/all_to_all | solution.py:68
  287.9 32.7 %all-to-all-start.5 = ((bf16[3,2048,128]{2,0,1:T(4,128)(2,1)}), bf16[3,2048,128]{2,0,1:T(4,128)(2,1)}, u32[]{:S(2)}, u32[]{:S(2)}) async-start(bf16[3,2048,128]{2,0,1:T(4,128)(2,1)} %copy.84), calls=%async_computation.5 | async-start | bytes 4194304 | tf_op jit(solution)/shard_map/all_to_all | solution.py:69
  320.6 5.2 copy-start.9
  320.6 74.7 %all-to-all-start.2 = ((bf16[6,2048,128]{2,0,1:T(8,128)(2,1)}), bf16[6,2048,128]{2,0,1:T(8,128)(2,1)}, u32[]{:S(2)}, u32[]{:S(2)}) async-start(bf16[6,2048,128]{2,0,1:T(8,128)(2,1)} %copy.74), calls=%async_computation.2 | async-start | bytes 8388608 | tf_op jit(solution)/shard_map/all_to_all | solution.py:68
  325.8 16.4 %copy-start.11 = (bf16[6,512,128]{1,2,0:T(8,128)(2,1)S(1)}, bf16[6,512,128]{1,2,0:T(8,128)(2,1)}, u32[]{:S(2)}) copy-start(bf16[6,512,128]{1,2,0:T(8,128)(2,1)} %get-tuple-element.33) | copy-start | bytes 2359300
  395.3 55.6 %all-to-all-start.3 = ((bf16[6,2048,128]{2,0,1:T(8,128)(2,1)}), bf16[6,2048,128]{2,0,1:T(8,128)(2,1)}, u32[]{:S(2)}, u32[]{:S(2)}) async-start(bf16[6,2048,128]{2,0,1:T(8,128)(2,1)} %copy.76), calls=%async_computation.3 | async-start | bytes 8388608 | tf_op jit(solution)/shard_map/all_to_all | solution.py:69
  510.6 100.2 %all-to-all-start.6 = ((bf16[1,4,512,2048]{3,2,0,1:T(8,128)(2,1)}), bf16[1,4,512,2048]{3,2,0,1:T(8,128)(2,1)}, u32[]{:S(2)}, u32[]{:S(2)}) async-start(bf16[1,4,512,2048]{3,2,0,1:T(8,128)(2,1)} %maximum_bitcast_fusion), calls=%async_computation.6 | async-start | bytes 16777216 | tf_op jit(solution)/shard_map/all_to_all | solution.py:161
  635.4 30.3 %all-to-all-start.7 = ((bf16[2,512,512]{1,0,2:T(2,128)(2,1)}), bf16[2,512,512]{1,0,2:T(2,128)(2,1)S(1)}, u32[]{:S(2)}, u32[]{:S(2)}) async-start(bf16[2,512,512]{1,0,2:T(2,128)(2,1)} %copy.87), calls=%async_computation.7 | async-start | bytes 2097152 | tf_op jit(solution)/shard_map/all_to_all | solution.py:46
  661.2 8.0 %copy-start.3 = (f32[512,128]{1,0:T(8,128)S(1)}, f32[512,128]{1,0:T(8,128)}, u32[]{:S(2)}) copy-start(f32[512,128]{1,0:T(8,128)} %get-tuple-element.5) | copy-start | bytes 786436
  665.7 20.7 %all-to-all-start.8 = ((bf16[2,512,512]{1,0,2:T(2,128)(2,1)}), bf16[2,512,512]{1,0,2:T(2,128)(2,1)S(1)}, u32[]{:S(2)}, u32[]{:S(2)}) async-start(bf16[2,512,512]{1,0,2:T(2,128)(2,1)} %copy.90), calls=%async_computation.8 | async-start | bytes 2097152 | tf_op jit(solution)/shard_map/all_to_all | solution.py:45
  669.2 96.3 %all-reduce.2.cloned.1.call-start = ((), (), s32[]{:S(2)}) async-start(), calls=%async_computation.9 | async-start | bytes 1048576 | tf_op jit(solution)/shard_map/psum | solution.py:170
  (3 other events, 2.8 us)
Sparse Core Ops, SparseCore 0:
  735.9 29.5 all-reduce.1
where the time goes:
time: 784 us; the launch traced here: 775 us
  matrix products  448 us (57%)
  waiting for transfers between devices  123 us (16%)
  other arithmetic  61.5 us (8%)
  local copies, waits for them, and re-layouts  54.4 us (7%)
  starting transfers between devices  40.7 us (5%)
  blocking collectives  32.9 us (4%)
  between operations  14.3 us (2%)
    all_to_all x1, waiting for transfers between devices, body(): lax.all_to_all(products[None], 'field', split_axis=1, concat_axis=0, tile...  93.2 us
    dot_general x2, matrix products, inverse(): jnp.dot(flat_im, isin.T, preferred_element_type=jnp.float32)  46.6 us
    dot_general x2, matrix products, inverse(): jnp.dot(flat_re, icos.T, preferred_element_type=jnp.float32)  44 us
    dot_general x2, matrix products, column_part(): jnp.dot(flat, cos_t, preferred_element_type=jnp.float32)  41 us
    dot_general x2, matrix products, inverse(): jnp.einsum('yk,mkj->myj', isin, z_re, preferred_element_type=jnp.float32)  40.5 us
    dot_general x2, matrix products, column_part(): jnp.dot(flat, sin_t, preferred_element_type=jnp.float32)  38.1 us
    dot_general x2, matrix products, inverse(): jnp.einsum('yk,mkj->myj', isin, z_im, preferred_element_type=jnp.float32)  37.2 us
    dot_general x2, matrix products, inverse(): jnp.einsum('yk,mkj->myj', icos, z_re, preferred_element_type=jnp.float32)  36.1 us
  transfers between devices with their start and end apart: 10, of which 2 were waited for; matrix products, arithmetic and copies ran while one was open for 38% of the time, Pallas kernels for 0%

commit v1 on v0

--- a/solution.py
+++ b/solution.py
@@ -5,6 +5,28 @@
 from jax.sharding import PartitionSpec as P
 
 TILE = 128
+
+
+def cut_along(x, dim, peers):
+    before, after = (x.shape[:dim], x.shape[dim + 1 :])
+    return jnp.moveaxis(x.reshape(*before, peers, -1, *after), dim, 0)
+
+
+def joined_along(blocks, dim):
+    dims = list(blocks.shape[1:])
+    dims[dim] *= blocks.shape[0]
+    return jnp.moveaxis(blocks, 0, dim).reshape(dims)
+
+
+def pairwise_exchange(x, axis, split_dim, concat_dim):
+    length, here = (lax.axis_size(axis), lax.axis_index(axis))
+    blocks = cut_along(x, split_dim, length)
+    outs = [blocks[here]]
+    for step in range(1, length):
+        sent = blocks[here ^ step]
+        outs.append(lax.ppermute(sent, axis, [(i, i ^ step) for i in range(length)]))
+    blocks = jnp.stack(outs)[here ^ jnp.arange(length)]
+    return joined_along(blocks, concat_dim)
 
 
 def tables(npix, kf, scale):
@@ -66,7 +88,7 @@
     ).astype(jnp.bfloat16)
     y_re, y_im = (
         lax.all_to_all(y_re, "rows", split_axis=1, concat_axis=2, tiled=True),
-        lax.all_to_all(y_im, "rows", split_axis=1, concat_axis=2, tiled=True),
+        pairwise_exchange(y_im, "rows", 1, 2),
     )
     height = y_re.shape[1]
     flat_re = y_re.reshape(count * height, -1)

time: 784 us -> 824 us (1.051)
  local copies, waits for them, and re-layouts: 54.4 us -> 97.5 us
    unnamed x35 -> x63, local copies, waits for them, and re-layouts: 3.42 us -> 22.2 us
    another operation x0 -> x2, local copies, waits for them, and re-layouts: none -> 14.9 us
    convert_element_type x2 -> x0, local copies, waits for them, and re-layouts: 10.5 us -> none  [inverse(): y_im = (jnp.einsum('yk,mkj->myj', icos, z_im, preferred_element_type=jnp....]
    all_to_all x2 -> x0, starting transfers between devices: 9.3 us -> none  [inverse(): lax.all_to_all(y_im, 'rows', split_axis=1, concat_axis=2, tiled=True)]
    reshape x0 -> x2, local copies, waits for them, and re-layouts: none -> 8.67 us  [cut_along(): return jnp.moveaxis(x.reshape(*before, peers, -1, *after), dim, 0)]
  transfers between devices with their start and end apart: 10 -> 14, of which waited for: 2 -> 3; matrix products, arithmetic and copies ran while one was open for 38% -> 30% of each run, Pallas kernels for 0% -> 0%
where the time goes in v1:
time: 824 us; the launch traced here: 815 us
  matrix products  442 us (54%)
  waiting for transfers between devices  123 us (15%)
  local copies, waits for them, and re-layouts  97.5 us (12%)
  other arithmetic  64.7 us (8%)
  starting transfers between devices  36.6 us (4%)
  blocking collectives  35.4 us (4%)
  between operations  14.7 us (2%)
    all_to_all x1, waiting for transfers between devices, body(): lax.all_to_all(products[None], 'field', split_axis=1, concat_axis=0, tile...  93.2 us
    dot_general x2, matrix products, inverse(): jnp.dot(flat_im, isin.T, preferred_element_type=jnp.float32)  44.5 us
    dot_general x2, matrix products, inverse(): jnp.dot(flat_re, icos.T, preferred_element_type=jnp.float32)  41.2 us
    dot_general x2, matrix products, column_part(): jnp.dot(flat, cos_t, preferred_element_type=jnp.float32)  41 us
    dot_general x2, matrix products, inverse(): jnp.einsum('yk,mkj->myj', isin, z_re, preferred_element_type=jnp.float32)  40.5 us
    dot_general x2, matrix products, column_part(): jnp.dot(flat, sin_t, preferred_element_type=jnp.float32)  37.9 us
    dot_general x2, matrix products, inverse(): jnp.einsum('yk,mkj->myj', isin, z_im, preferred_element_type=jnp.float32)  37.9 us
    dot_general x2, matrix products, inverse(): jnp.einsum('yk,mkj->myj', icos, z_re, preferred_element_type=jnp.float32)  35.7 us
  transfers between devices with their start and end apart: 14, of which 3 were waited for; matrix products, arithmetic and copies ran while one was open for 30% of the time, Pallas kernels for 0%

profile of v1, /device:TPU:0, one launch (start us, length us, event | category | flops | bytes accessed | tf_op | source)
XLA Modules:
  0.0 814.7 jit_solution(5742021586027879278)
XLA Ops:
  10.6 16.8 %negate_convert_fusion.1 = bf16[1024,512]{1,0:T(8,128)(2,1)S(1)} fusion(bf16[1024,2048]{1,0:T(8,128)(2,1)S(1)} %bitcast.302, s32[512]{0:T(512)S(1)} %iota_add_fusion), kind=kOutput, calls=%fused_computation.87 | convolution fusion | flops 2165309440 | bytes 5244928 | tf_op jit(solution)/shard_map/dot_general | solution.py:58
  34.0 18.9 %fusion.65 = bf16[1024,512]{1,0:T(8,128)(2,1)S(1)} fusion(bf16[1024,2048]{1,0:T(8,128)(2,1)} %bitcast.303, s32[512]{0:T(512)S(1)} %iota_add_fusion), kind=kOutput, calls=%fused_computation.98 | convolution fusion | flops 2164785152 | bytes 5244928 | tf_op jit(solution)/shard_map/dot_general | solution.py:53
  55.8 16.3 %select_reduce_fusion.2 = (f32[512,128]{1,0:T(8,128)}, f32[512,128]{1,0:T(8,128)S(1)}, f32[512,128]{1,0:T(8,128)S(1)}) fusion(f32[64]{0:T(128)S(1)} %copy-done.22, s32[512,128]{1,0:T(8,128)S(1)} %copy-done.12, f32[64]{0:T(128)S(1)} %get-tuple-element.12, f32[64]{0:T(128)S(1)} %get-tuple-element.13), kind=kLoop, calls=%fused_computation.5 | loop fusion | flops 29163520 | bytes 1049344 | tf_op jit(solution)/shard_map/reduce_sum | solution.py:120
  98.5 16.3 %fusion.44 = f32[2,128,512]{2,1,0:T(8,128)S(1)} fusion(bf16[2,2048,128]{1,2,0:T(8,128)(2,1)S(1)} %all_to_all.84, s32[512]{0:T(512)S(1)} %iota_add_fusion), kind=kOutput, calls=%fused_computation.75 | convolution fusion | flops 553648128 | bytes 1574912 | tf_op jit(solution)/shard_map/yk,myj->mkj/dot_general | solution.py:73
  148.2 19.5 %fusion.38 = f32[6,128,2048]{2,1,0:T(8,128)} fusion(bf16[6,512,128]{1,2,0:T(8,128)(2,1)S(1)} %get-tuple-element.41, s32[512]{0:T(512)S(1)} %iota_add_fusion), kind=kOutput, calls=%fused_computation.69 | convolution fusion | flops 1627389952 | bytes 7079936 | tf_op jit(solution)/shard_map/yk,mkj->myj/dot_general | solution.py:82
  167.9 16.7 %fusion.36 = f32[6,128,2048]{2,1,0:T(8,128)S(1)} fusion(bf16[6,512,128]{1,2,0:T(8,128)(2,1)S(1)} %fusion.125, s32[512]{0:T(512)S(1)} %iota_add_fusion), kind=kOutput, calls=%fused_computation.67 | convolution fusion | flops 1627389952 | bytes 7079936 | tf_op jit(solution)/shard_map/yk,mkj->myj/dot_general | solution.py:86
  184.6 22.0 %fusion.21 = bf16[6,2048,128]{1,2,0:T(8,128)(2,1)} fusion(f32[6,128,2048]{2,1,0:T(8,128)S(1)} %fusion.36, bf16[6,512,128]{1,2,0:T(8,128)(2,1)S(1)} %get-tuple-element.41, s32[512]{0:T(512)S(1)} %iota_add_fusion), kind=kOutput, calls=%fused_computation.51 | convolution fusion | flops 1630535680 | bytes 10225664 | tf_op jit(solution)/shard_map/yk,mkj->myj/dot_general | solution.py:87
  213.0 19.0 %all_gather.6 = bf16[4,512,128]{2,1,0:T(8,128)(2,1)} all-gather(bf16[1,512,128]{2,1,0:T(8,128)(2,1)} %copy.101), channel_id=1, replica_groups=mesh['real'=4,'rows'=4,'field'=2] {'real'}, dimensions={0}, use_global_device_ids=true | all-gather | bytes 655360 | tf_op jit(solution)/shard_map/all_gather | solution.py:162
  232.8 16.4 %all_gather.7 = bf16[4,512,128]{2,1,0:T(8,128)(2,1)S(1)} all-gather(bf16[1,512,128]{2,1,0:T(8,128)(2,1)} %copy.103), channel_id=1, replica_groups=mesh['real'=4,'rows'=4,'field'=2] {'real'}, dimensions={0}, use_global_device_ids=true | all-gather | bytes 655360 | tf_op jit(solution)/shard_map/all_gather | solution.py:168
  256.2 16.2 %fusion.34 = f32[3,128,2048]{2,1,0:T(8,128)S(1)} fusion(s32[512]{0:T(512)S(1)} %iota_add_fusion, bf16[1,512,128]{1,2,0:T(8,128)(2,1)S(1)} %get-tuple-element.33, bf16[1,512,128]{1,2,0:T(8,128)(2,1)S(1)} %get-tuple-element.32, bf16[1,512,128]{1,2,0:T(8,128)(2,1)S(1)} %get-tuple-element.44), kind=kOutput, calls=%fused_computation.65 | convolution fusion | flops 822476800 | bytes 3540992 | tf_op jit(solution)/shard_map/yk,mkj->myj/dot_general | solution.py:82
  272.4 17.3 %fusion.32 = f32[3,128,2048]{2,1,0:T(8,128)} fusion(s32[512]{0:T(512)S(1)} %iota_add_fusion, bf16[1,512,128]{1,2,0:T(8,128)(2,1)S(1)} %get-tuple-element.42, bf16[1,512,128]{1,2,0:T(8,128)(2,1)S(1)} %get-tuple-element.43, bf16[1,512,128]{1,2,0:T(8,128)(2,1)S(1)} %get-tuple-element.45), kind=kOutput, calls=%fused_computation.63 | convolution fusion | flops 822476800 | bytes 3540992 | tf_op jit(solution)/shard_map/yk,mkj->myj/dot_general | solution.py:86
  289.8 17.4 %fusion.22 = bf16[3,2048,128]{1,2,0:T(8,128)(2,1)} fusion(f32[3,128,2048]{2,1,0:T(8,128)S(1)} %fusion.34, s32[512]{0:T(512)S(1)} %iota_add_fusion, bf16[1,512,128]{1,2,0:T(8,128)(2,1)S(1)} %get-tuple-element.42, bf16[1,512,128]{1,2,0:T(8,128)(2,1)S(1)} %get-tuple-element.43, bf16[1,512,128]{1,2,0:T(8,128)(2,1)S(1)} %get-tuple-element.45), kind=kOutput, calls=%fused_computation.53 | convolution fusion | flops 824049664 | bytes 5113856 | tf_op jit(solution)/shard_map/yk,mkj->myj/dot_general | solution.py:83
  316.2 18.6 %fusion.23 = bf16[3,2048,128]{1,2,0:T(8,128)(2,1)} fusion(f32[3,128,2048]{2,1,0:T(8,128)} %fusion.32, s32[512]{0:T(512)S(1)} %iota_add_fusion, bf16[1,512,128]{1,2,0:T(8,128)(2,1)S(1)} %copy-done.14, bf16[1,512,128]{1,2,0:T(8,128)(2,1)S(1)} %get-tuple-element.32, bf16[1,512,128]{1,2,0:T(8,128)(2,1)S(1)} %copy-done.16), kind=kOutput, calls=%fused_computation.54 | convolution fusion | flops 824049664 | bytes 5113856 | tf_op jit(solution)/shard_map/yk,mkj->myj/dot_general | solution.py:87
  376.1 20.5 %fusion.20 = bf16[6,2048,128]{1,2,0:T(8,128)(2,1)} fusion(f32[6,128,2048]{2,1,0:T(8,128)} %fusion.38, bf16[6,512,128]{1,2,0:T(8,128)(2,1)} %copy-done.19, s32[512]{0:T(512)S(1)} %iota_add_fusion), kind=kOutput, calls=%fused_computation.50 | convolution fusion | flops 1630535680 | bytes 10225664 | tf_op jit(solution)/shard_map/yk,mkj->myj/dot_general | solution.py:83
  430.0 17.3 %fusion.60 = f32[1536,2048]{1,0:T(8,128)S(1)} fusion(s32[512]{0:T(512)S(1)} %iota_add_fusion, bf16[192,8,4,128]{3,2,1,0:T(4,128)(2,1)S(1)} %bitcast.317), kind=kOutput, calls=%fused_computation.92 | convolution fusion | flops 3238002688 | bytes 14157824 | tf_op jit(solution)/shard_map/dot_general | solution.py:96
  447.3 20.8 %fusion = f32[1536,2048]{1,0:T(8,128)} fusion(f32[1536,2048]{1,0:T(8,128)S(1)} %fusion.60, s32[512]{0:T(512)S(1)} %iota_add_fusion, bf16[192,8,4,128]{3,2,1,0:T(4,128)(2,1)S(1)} %bitcast.318), kind=kOutput, calls=%fused_computation.9 | convolution fusion | flops 3247439872 | bytes 26740736 | tf_op jit(solution)/shard_map/dot_general | solution.py:96
  472.7 23.9 %fusion.17 = f32[3072,2048]{1,0:T(8,128)} fusion(bf16[384,8,4,128]{3,2,1,0:T(4,128)(2,1)S(1)} %bitcast.311, s32[512]{0:T(512)S(1)} %iota_add_fusion), kind=kOutput, calls=%fused_computation.44 | convolution fusion | flops 6459228160 | bytes 28313600 | tf_op jit(solution)/shard_map/dot_general | solution.py:96
  496.6 23.7 %subtract_convert_fusion = bf16[3072,2048]{1,0:T(8,128)(2,1)S(1)} fusion(f32[3072,2048]{1,0:T(8,128)} %fusion.17, bf16[384,8,4,128]{3,2,1,0:T(4,128)(2,1)S(1)} %bitcast.312, s32[512]{0:T(512)S(1)} %iota_add_fusion), kind=kOutput, calls=%fused_computation.2 | convolution fusion | flops 6471811072 | bytes 40896512 | tf_op jit(solution)/shard_map/dot_general | solution.py:96
  558.3 93.2 %all-to-all-done.4 = bf16[1,4,512,2048]{3,2,0,1:T(8,128)(2,1)} async-done(((bf16[1,4,512,2048]{3,2,0,1:T(8,128)(2,1)}), bf16[1,4,512,2048]{3,2,0,1:T(8,128)(2,1)}, u32[]{:S(2)}, u32[]{:S(2)}) %all-to-all-start.4) | async-done | bytes 8388640 | tf_op jit(solution)/shard_map/all_to_all | solution.py:183
  651.5 21.1 %negate_convert_fusion = bf16[2048,512]{1,0:T(8,128)(2,1)S(1)} fusion(bf16[2048,2048]{1,0:T(8,128)(2,1)} %bitcast.50, s32[512]{0:T(512)S(1)} %iota_add_fusion), kind=kOutput, calls=%fused_computation.33 | convolution fusion | flops 4313841664 | bytes 10487808 | tf_op jit(solution)/shard_map/dot_general | solution.py:58
  679.8 22.1 %convolution_convert_fusion = bf16[2048,512]{1,0:T(8,128)(2,1)} fusion(bf16[2048,2048]{1,0:T(8,128)(2,1)} %bitcast.50, s32[512]{0:T(512)S(1)} %iota_add_fusion), kind=kOutput, calls=%fused_computation.52 | convolution fusion | flops 4312793088 | bytes 10487808 | tf_op jit(solution)/shard_map/dot_general | solution.py:53
  710.7 16.8 %fusion.40 = f32[2,128,512]{2,1,0:T(8,128)} fusion(bf16[2,2048,128]{1,2,0:T(8,128)(2,1)S(1)} %bitcast.320, s32[512]{0:T(512)S(1)} %iota_add_fusion), kind=kOutput, calls=%fused_computation.71 | convolution fusion | flops 553648128 | bytes 1574912 | tf_op jit(solution)/shard_map/yk,myj->mkj/dot_general | solution.py:70
  727.8 16.1 %fusion.42 = f32[2,128,512]{2,1,0:T(8,128)S(1)} fusion(bf16[2,2048,128]{1,2,0:T(8,128)(2,1)S(1)} %bitcast.322, s32[512]{0:T(512)S(1)} %iota_add_fusion), kind=kOutput, calls=%fused_computation.73 | convolution fusion | flops 553648128 | bytes 1574912 | tf_op jit(solution)/shard_map/yk,myj->mkj/dot_general | solution.py:73
  777.1 28.0 %all-reduce.2.cloned.1.call-done = bf16[1,2,2,512,128]{3,4,1,2,0:T(8,128)(2,1)} async-done(((bf16[1,2,2,512,128]{3,4,1,2,0:T(8,128)(2,1)}), bf16[1,2,2,512,128]{3,4,1,2,0:T(8,128)(2,1)}) %all-reduce.2.cloned.1.call-update) | async-done | bytes 524304 | tf_op jit(solution)/shard_map/psum | solution.py:192
  (158 shorter events, 265.0 us)
Async XLA Ops:
  10.6 16.8 %copy-start.3 = (bf16[2,512,2048]{2,1,0:T(8,128)(2,1)}, bf16[2,512,2048]{2,1,0:T(8,128)(2,1)S(1)}, u32[]{:S(2)}) copy-start(bf16[2,512,2048]{2,1,0:T(8,128)(2,1)S(1)} %maximum_select_fusion) | copy-start | bytes 12582916
  29.5 42.5 %all-to-all-start.1 = ((bf16[2,512,512]{1,0,2:T(2,128)(2,1)}), bf16[2,512,512]{1,0,2:T(2,128)(2,1)S(1)}, u32[]{:S(2)}, u32[]{:S(2)}) async-start(bf16[2,512,512]{1,0,2:T(2,128)(2,1)} %copy.91), calls=%async_computation.1 | async-start | bytes 2097152 | tf_op jit(solution)/shard_map/all_to_all | solution.py:68
  33.9 21.1 %copy-start.23 = (f32[1,64]{1,0:T(1,128)S(1)}, f32[1,64]{1,0:T(1,128)}, u32[]{:S(2)}) copy-start(f32[1,64]{1,0:T(1,128)} %param.12) | copy-start | bytes 772
  33.9 21.1 %copy-start.24 = (f32[1,64]{1,0:T(1,128)S(1)}, f32[1,64]{1,0:T(1,128)}, u32[]{:S(2)}) copy-start(f32[1,64]{1,0:T(1,128)} %param.13) | copy-start | bytes 772
  34.0 21.1 %copy-start.25 = (s32[4]{0:T(128)S(1)}, s32[4]{0:T(128)}, u32[]{:S(2)}) copy-start(s32[4]{0:T(128)} %param.15) | copy-start | bytes 52
  34.0 21.8 %copy-start.12 = (s32[512,128]{1,0:T(8,128)S(1)}, s32[512,128]{1,0:T(8,128)}, u32[]{:S(2)}) copy-start(s32[512,128]{1,0:T(8,128)} %param.11) | copy-start | bytes 786436
  34.0 21.8 %copy-start.22 = (f32[64]{0:T(128)S(1)}, f32[64]{0:T(128)}, u32[]{:S(2)}) copy-start(f32[64]{0:T(128)} %param.14) | copy-start | bytes 772
  52.9 202.1 %copy-start.17 = (f32[512]{0:T(512)}, f32[512]{0:T(512)S(1)}, u32[]{:S(2)}) copy-start(f32[512]{0:T(512)S(1)} %convert_multiply_fusion) | copy-start | bytes 6148
  55.0 200.0 %copy-start.20 = (f32[128]{0:T(128)}, f32[128]{0:T(128)S(1)}, u32[]{:S(2)}) copy-start(f32[128]{0:T(128)S(1)} %convert_multiply_fusion.1) | copy-start | bytes 1540
  72.1 24.8 %all-to-all-start = ((bf16[2,512,512]{1,0,2:T(2,128)(2,1)}), bf16[2,512,512]{1,0,2:T(2,128)(2,1)S(1)}, u32[]{:S(2)}, u32[]{:S(2)}) async-start(bf16[2,512,512]{1,0,2:T(2,128)(2,1)} %copy.89), calls=%async_computation | async-start | bytes 2097152 | tf_op jit(solution)/shard_map/all_to_all | solution.py:67
  77.1 70.9 %copy-start = (f32[512,128]{0,1:T(8,128)}, f32[512,128]{0,1:T(8,128)S(1)}, u32[]{:S(2)}) copy-start(f32[512,128]{0,1:T(8,128)S(1)} %copy.88) | copy-start | bytes 786436
  311.4 101.5 %all-to-all-start.3 = ((bf16[3,2048,128]{2,0,1:T(4,128)(2,1)}), bf16[3,2048,128]{2,0,1:T(4,128)(2,1)}, u32[]{:S(2)}, u32[]{:S(2)}) async-start(bf16[3,2048,128]{2,0,1:T(4,128)(2,1)} %copy.105), calls=%async_computation.3 | async-start | bytes 4194304 | tf_op jit(solution)/shard_map/all_to_all | solution.py:90
  348.7 27.1 %collective-permute-start.5 = (bf16[3,512,128]{2,1,0:T(8,128)(2,1)}, bf16[3,512,128]{2,1,0:T(8,128)(2,1)}, u32[]{:S(2)}, u32[]{:S(2)}) collective-permute-start(bf16[3,512,128]{2,1,0:T(8,128)(2,1)} %bitcast.331), channel_id=1, source_target_pairs={{0,6},{2,4},{4,2},{6,0},{1,7},{3,5},{5,3},{7,1},{8,14},{10,12},{12... | collective-permute-start | bytes 1179656 | tf_op jit(solution)/shard_map/ppermute | solution.py:27
  363.1 54.7 %collective-permute-start.2 = (bf16[6,512,128]{2,1,0:T(8,128)(2,1)}, bf16[6,512,128]{2,1,0:T(8,128)(2,1)}, u32[]{:S(2)}, u32[]{:S(2)}) collective-permute-start(bf16[6,512,128]{2,1,0:T(8,128)(2,1)} %bitcast.326), channel_id=1, source_target_pairs={{0,6},{2,4},{4,2},{6,0},{1,7},{3,5},{5,3},{7,1},{8,14},{10,12},{12... | collective-permute-start | bytes 2359304 | tf_op jit(solution)/shard_map/ppermute | solution.py:27
  367.8 50.0 %collective-permute-start.1 = (bf16[6,512,128]{2,1,0:T(8,128)(2,1)}, bf16[6,512,128]{2,1,0:T(8,128)(2,1)}, u32[]{:S(2)}, u32[]{:S(2)}) collective-permute-start(bf16[6,512,128]{2,1,0:T(8,128)(2,1)} %bitcast.327), channel_id=1, source_target_pairs={{0,4},{2,6},{4,0},{6,2},{1,5},{3,7},{5,1},{7,3},{8,12},{10,14},{12... | collective-permute-start | bytes 2359304 | tf_op jit(solution)/shard_map/ppermute | solution.py:27
  372.4 45.4 %collective-permute-start = (bf16[6,512,128]{2,1,0:T(8,128)(2,1)}, bf16[6,512,128]{2,1,0:T(8,128)(2,1)}, u32[]{:S(2)}, u32[]{:S(2)}) collective-permute-start(bf16[6,512,128]{2,1,0:T(8,128)(2,1)} %bitcast.328), channel_id=1, source_target_pairs={{0,2},{2,0},{4,6},{6,4},{1,3},{3,1},{5,7},{7,5},{8,10},{10,8},{12,... | collective-permute-start | bytes 2359304 | tf_op jit(solution)/shard_map/ppermute | solution.py:27
  374.0 34.4 %collective-permute-start.4 = (bf16[3,512,128]{2,1,0:T(8,128)(2,1)}, bf16[3,512,128]{2,1,0:T(8,128)(2,1)S(1)}, u32[]{:S(2)}, u32[]{:S(2)}) collective-permute-start(bf16[3,512,128]{2,1,0:T(8,128)(2,1)} %bitcast.41), channel_id=1, source_target_pairs={{0,4},{2,6},{4,0},{6,2},{1,5},{3,7},{5,1},{7,3},{8,12},{10,14},{12... | collective-permute-start | bytes 1179656 | tf_op jit(solution)/shard_map/ppermute | solution.py:27
  375.8 32.6 %collective-permute-start.3 = (bf16[3,512,128]{2,1,0:T(8,128)(2,1)}, bf16[3,512,128]{2,1,0:T(8,128)(2,1)S(1)}, u32[]{:S(2)}, u32[]{:S(2)}) collective-permute-start(bf16[3,512,128]{2,1,0:T(8,128)(2,1)} %bitcast.39), channel_id=1, source_target_pairs={{0,2},{2,0},{4,6},{6,4},{1,3},{3,1},{5,7},{7,5},{8,10},{10,8},{12,... | collective-permute-start | bytes 1179656 | tf_op jit(solution)/shard_map/ppermute | solution.py:27
  412.8 55.2 %all-to-all-start.2 = ((bf16[6,2048,128]{2,0,1:T(8,128)(2,1)}), bf16[6,2048,128]{2,0,1:T(8,128)(2,1)}, u32[]{:S(2)}, u32[]{:S(2)}) async-start(bf16[6,2048,128]{2,0,1:T(8,128)(2,1)} %copy.94), calls=%async_computation.2 | async-start | bytes 8388608 | tf_op jit(solution)/shard_map/all_to_all | solution.py:90
  430.0 17.3 %copy-start.8 = (bf16[3,512,4,128]{3,2,1,0:T(4,128)(2,1)S(1)}, bf16[3,512,4,128]{3,2,1,0:T(4,128)(2,1)}, u32[]{:S(2)}) copy-start(bf16[3,512,4,128]{3,2,1,0:T(4,128)(2,1)} %copy.111) | copy-start | bytes 4718596
  551.3 100.2 %all-to-all-start.4 = ((bf16[1,4,512,2048]{3,2,0,1:T(8,128)(2,1)}), bf16[1,4,512,2048]{3,2,0,1:T(8,128)(2,1)}, u32[]{:S(2)}, u32[]{:S(2)}) async-start(bf16[1,4,512,2048]{3,2,0,1:T(8,128)(2,1)} %maximum_bitcast_fusion), calls=%async_computation.4 | async-start | bytes 16777216 | tf_op jit(solution)/shard_map/all_to_all | solution.py:183
  675.8 30.5 %all-to-all-start.5 = ((bf16[2,512,512]{1,0,2:T(2,128)(2,1)}), bf16[2,512,512]{1,0,2:T(2,128)(2,1)S(1)}, u32[]{:S(2)}, u32[]{:S(2)}) async-start(bf16[2,512,512]{1,0,2:T(2,128)(2,1)} %copy.113), calls=%async_computation.5 | async-start | bytes 2097152 | tf_op jit(solution)/shard_map/all_to_all | solution.py:68
  706.4 21.1 %all-to-all-start.6 = ((bf16[2,512,512]{1,0,2:T(2,128)(2,1)}), bf16[2,512,512]{1,0,2:T(2,128)(2,1)S(1)}, u32[]{:S(2)}, u32[]{:S(2)}) async-start(bf16[2,512,512]{1,0,2:T(2,128)(2,1)} %copy.116), calls=%async_computation.6 | async-start | bytes 2097152 | tf_op jit(solution)/shard_map/all_to_all | solution.py:67
  709.9 95.2 %all-reduce.2.cloned.1.call-start = ((), (), s32[]{:S(2)}) async-start(), calls=%async_computation.7 | async-start | bytes 1048576 | tf_op jit(solution)/shard_map/psum | solution.py:192
  (17 other events, 198.6 us)
Sparse Core Ops, SparseCore 0:
  777.2 27.8 all-reduce.1
